TPU v7x, 256 devices: a whole 4x4x8 slice. The times are simulated.
256 devices in a mesh: seq: 32 (over x, y, core), tensor: 8 (over z).
Axes of the slice: x: 4, y: 4, z: 8, core: 2. Of those that a mesh axis runs over, the one named last changes fastest.
Arguments:
- tokens: bfloat16 [4, 4, 1600], replicated, may hold values from -6 to 6
- first_gain: float32 [1600], replicated, may hold values from 0.25 to 1.75
- first_shift: float32 [1600], replicated, may hold values from -3 to 3
- input_weight: bfloat16 [1600, 3, 2048], P(None, None, 'tensor'), may hold values from -0.15625 to 0.15625
- input_bias: float32 [3, 2048], P(None, 'tensor')
- output_weight: bfloat16 [2048, 1600], P('tensor'), may hold values from -0.125 to 0.125
- output_bias: float32 [1600], replicated, may hold values from -3 to 3
- second_gain: float32 [1600], replicated, may hold values from 0.25 to 1.75
- second_shift: float32 [1600], replicated, may hold values from -3 to 3
- expand_weight: bfloat16 [1600, 6400], P(None, 'tensor'), may hold values from -0.15625 to 0.15625
- expand_bias: float32 [6400], P('tensor'), may hold values from -3 to 3
- contract_weight: bfloat16 [6400, 1600], P('tensor'), may hold values from -0.078125 to 0.078125
- contract_bias: float32 [1600], replicated, may hold values from -3 to 3
- key_cache: bfloat16 [4, 16384, 2048], P(None, 'seq', 'tensor')
- value_cache: bfloat16 [4, 16384, 2048], P(None, 'seq', 'tensor'), may hold values from -6 to 6
- cache_fill: int32 [4, 32], replicated, may hold values from 0 to 508, as said below
- owner_shard: int32 [4, 4], replicated, may hold values from 0 to 31, as said below
Outputs:
- hidden_out: bfloat16 [4, 4, 1600], replicated
- new_keys: bfloat16 [4, 16384, 2048], P(None, 'seq', 'tensor')
- new_values: bfloat16 [4, 16384, 2048], P(None, 'seq', 'tensor')
Inputs may be any that keep to these rules, and one draw needn't show every extreme that they name: `cache_fill`: 1 request hold 506 to 508 entries on every shard; every other request holds 1 to 508 entries on one shard and none on the others. `owner_shard`: a request with entries on one shard only appends all its new tokens to that shard.
All inputs are finite; a program needn't handle non-finite values.
Results may differ from a plain program's by a relative error of at most 0.0046.
Values sent between devices are 32-bit elements; how exact they have to be, the bound alone decides.
A program may use at most 64 MiB of HBM per device.

v0:
```python
import math

import jax
import jax.numpy as jnp
from jax import lax
from jax.sharding import PartitionSpec as P

HEAD_DIM = 64


def layer_norm(values, gain, shift):
    center = values - jnp.mean(values, axis=-1, keepdims=True)
    spread = jnp.mean(center * center, axis=-1, keepdims=True)
    return center * lax.rsqrt(spread + 1e-05) * gain + shift


def widen_heads(per_head):
    return jnp.repeat(per_head, HEAD_DIM, axis=-1)


def attend(queries, key_rows, value_rows, live_count):
    rounds, requests, row_width = queries.shape
    head_count = row_width // HEAD_DIM
    slot_count = key_rows.shape[1]
    query_heads = queries.reshape(rounds, requests, head_count, HEAD_DIM)
    key_heads = key_rows.reshape(requests, slot_count, head_count, HEAD_DIM)
    value_heads = value_rows.reshape(requests, slot_count, head_count, HEAD_DIM)
    scores = jnp.einsum(
        "tbhd,bshd->tbhs", query_heads, key_heads, preferred_element_type=jnp.float32
    ) * (1.0 / math.sqrt(HEAD_DIM))
    usable = (lax.iota(jnp.int32, slot_count)[None, None, :] < live_count[:, :, None])[
        :, :, None, :
    ]
    peaks = jnp.max(jnp.where(usable, scores, -1e30), axis=-1)
    weights = jnp.where(usable, jnp.exp(scores - peaks[..., None]), 0.0)
    totals = jnp.sum(weights, axis=-1)
    blended = jnp.einsum(
        "tbhs,bshd->tbhd",
        weights.astype(jnp.bfloat16),
        value_heads,
        preferred_element_type=jnp.float32,
    )
    return (peaks, totals, blended.reshape(rounds, requests, row_width))


def merge_heads(parts):
    peaks, totals, blended = parts
    highest = lax.pmax(peaks, "seq")
    factor = jnp.exp(peaks - highest)
    totals, blended = lax.psum((totals * factor, blended * widen_heads(factor)), "seq")
    return (blended / widen_heads(totals)).astype(jnp.bfloat16)


def project_in(rows, first_gain, first_shift, input_weight, input_bias):
    normed = layer_norm(rows.astype(jnp.float32), first_gain, first_shift).astype(jnp.bfloat16)
    packed = (
        jnp.einsum("rd,dch->rch", normed, input_weight, preferred_element_type=jnp.float32)
        + input_bias
    )
    return packed.astype(jnp.bfloat16)


def finish(
    rows,
    attended,
    output_weight,
    output_bias,
    second_gain,
    second_shift,
    expand_weight,
    expand_bias,
    contract_weight,
    contract_bias,
):
    heads_sum = lax.psum(
        jnp.dot(attended, output_weight, preferred_element_type=jnp.float32), "tensor"
    )
    middle = rows.astype(jnp.float32) + heads_sum + output_bias
    second = layer_norm(middle, second_gain, second_shift).astype(jnp.bfloat16)
    hidden = jax.nn.gelu(
        jnp.dot(second, expand_weight, preferred_element_type=jnp.float32) + expand_bias,
        approximate=True,
    ).astype(jnp.bfloat16)
    units_sum = lax.psum(
        jnp.dot(hidden, contract_weight, preferred_element_type=jnp.float32), "tensor"
    )
    return (units_sum + contract_bias + middle).astype(jnp.bfloat16)


def write_cache(cache, fresh_rows, slot_index, owned):
    slot_count = cache.shape[1]
    places = (lax.iota(jnp.int32, slot_count)[None, :] == slot_index[:, None]) & (
        owned[:, None] > 0
    )
    return jnp.where(places[:, :, None], fresh_rows[:, None, :], cache)


def per_device(
    tokens,
    first_gain,
    first_shift,
    input_weight,
    input_bias,
    output_weight,
    output_bias,
    second_gain,
    second_shift,
    expand_weight,
    expand_bias,
    contract_weight,
    contract_bias,
    key_cache,
    value_cache,
    cache_fill,
    owner_shard,
):
    shard = lax.axis_index("seq")
    shard_count = cache_fill.shape[1]
    picked = lax.iota(jnp.int32, shard_count)[None, :] == shard
    own_fill = jnp.sum(jnp.where(picked, cache_fill, 0), axis=1)
    owned = (owner_shard == shard).astype(jnp.int32)
    through = jnp.cumsum(owned, axis=0)
    slot_index = own_fill[None, :] + through - owned
    live_count = own_fill[None, :] + through
    step_total, requests, model_width = tokens.shape
    outputs = []
    for step_index in range(step_total):
        packed = project_in(tokens[step_index], first_gain, first_shift, input_weight, input_bias)
        key_cache = write_cache(key_cache, packed[:, 1], slot_index[step_index], owned[step_index])
        value_cache = write_cache(
            value_cache, packed[:, 2], slot_index[step_index], owned[step_index]
        )
        parts = attend(
            packed[None, :, 0], key_cache, value_cache, live_count[step_index : step_index + 1]
        )
        attended = merge_heads(parts)[0]
        outputs.append(
            finish(
                tokens[step_index],
                attended,
                output_weight,
                output_bias,
                second_gain,
                second_shift,
                expand_weight,
                expand_bias,
                contract_weight,
                contract_bias,
            )
        )
    hidden_out = jnp.stack(outputs)
    return (hidden_out, key_cache, value_cache)


def solution(mesh):
    return jax.shard_map(
        per_device,
        mesh=mesh,
        in_specs=(
            P(),
            P(),
            P(),
            P(None, None, "tensor"),
            P(None, "tensor"),
            P("tensor", None),
            P(),
            P(),
            P(),
            P(None, "tensor"),
            P("tensor"),
            P("tensor", None),
            P(),
            P(None, "seq", "tensor"),
            P(None, "seq", "tensor"),
            P(),
            P(),
        ),
        out_specs=(P(), P(None, "seq", "tensor"), P(None, "seq", "tensor")),
        check_vma=False,
    )
```

profile of v0, /device:TPU:1, one launch (start us, length us, event | category | flops | bytes accessed | tf_op | source)
XLA Modules:
  0.0 429.1 jit_solution(10217517019822369008)
XLA Ops:
  7.3 0.8 compare_convert_fusion
  8.2 1.1 convert_reduce_fusion
  9.3 1.0 fusion.28
  10.3 2.2 fusion.3
  12.6 0.5 fusion.2
  13.1 0.5 fusion.1
  13.5 2.3 copy.25
  15.8 2.2 fusion
  18.0 2.3 copy.24
  20.4 0.1 select_reduce_fusion.4
  20.9 4.8 %broadcast_select_fusion = (bf16[4,512,256]{1,2,0:T(8,128)(2,1)S(1)}, bf16[4,512,256]{1,2,0:T(8,128)(2,1)}, bf16[4,512,256]{1,2,0:T(8,128)(2,1)}, bf16[4,512,256...) fusion(pred[4,512]{1,0:T(4,128)(4,1)S(1)} %fusion.151, ...), kind=kLoop, calls=%fused_computation.12 | loop fusion | flops 4194304 | bytes 10510336 | tf_op jit(solution)/shard_map/jit(_where)/select_n | solution.py:95
  25.7 1.0 copy-done.3
  26.7 0.2 fusion.224
  27.1 0.7 fusion.147
  28.2 1.5 fusion.223
  29.9 1.3 fusion.146
  31.2 1.5 fusion.222
  32.7 1.3 fusion.145
  34.0 1.5 fusion.221
  35.6 1.3 fusion.144
  36.9 1.0 fusion.12
  37.8 66.8 %all-reduce.1 = (f32[1,4,4]{2,1,0:T(4,128)}, f32[1,4,4]{2,1,0:T(4,128)}, f32[1,4,4]{2,1,0:T(4,128)}, f32[1,4,4]{2,1,0:T(4,128)}) all-reduce(f32[1,4,4]{2,1,0:T(4,128)S(1)} %bitcast.321, f32[1,4,4]{2,1,0:T(4,128)S(1)} %bitcast.323, f32[1,4,4]{2,1,0:T(4,128)S(1)} %bitcast.322, ...), channel_id=1, replica_groups=mesh['seq'=32,'tensor'=8] {'seq'}, use_global_device_ids=true, to_apply=%region_38.39 | all-reduce | flops 64 | bytes 512 | tf_op jit(solution)/shard_map/pmax | solution.py:48
  104.6 1.3 fusion.178
  105.9 1.4 broadcast_multiply_fusion
  107.2 1.4 mul.328
  108.6 1.6 fusion.14
  110.2 1.3 fusion.181
  111.5 0.7 mul.312
  112.2 1.6 fusion.16
  113.8 1.3 fusion.184
  115.2 0.7 broadcast_multiply_fusion.2
  115.8 1.4 mul.296
  117.2 1.6 fusion.18
  118.8 1.3 fusion.187
  120.1 0.7 broadcast_multiply_fusion.3
  120.8 1.4 mul.279
  122.1 121.7 %all-reduce = (f32[1,4,256]{2,1,0:T(4,128)}, f32[4,4]{1,0:T(4,128)}, f32[1,4,256]{2,1,0:T(4,128)}, f32[4,4]{1,0:T(4,128)}, f32[1,4,256]{2,1,0:T(4,128)}, /*index...) all-reduce(f32[1,4,256]{2,1,0:T(4,128)} %mul.328, ...), channel_id=1, replica_groups=mesh['seq'=32,'tensor'=8] {'seq'}, use_global_device_ids=true, to_apply=%region_39.40 | all-reduce | flops 4160 | bytes 33280 | tf_op jit(solution)/shard_map/psum | solution.py:50
  243.9 1.4 broadcast_in_dim.307
  245.2 1.4 broadcast_in_dim.308
  246.6 1.3 broadcast_in_dim.298
  247.9 1.4 broadcast_in_dim.299
  249.3 1.3 broadcast_in_dim.289
  250.7 1.4 broadcast_in_dim.290
  252.0 1.3 broadcast_in_dim.280
  253.4 1.4 broadcast_in_dim.281
  254.7 1.6 fusion.176
  256.4 1.6 fusion.179
  258.0 1.6 fusion.182
  259.6 1.6 fusion.185
  261.3 70.7 %all-reduce.9.cloned.1.call-done = (f32[4,1600]{1,0:T(4,128)}, f32[4,1600]{1,0:T(4,128)}, f32[4,1600]{1,0:T(4,128)}, f32[4,1600]{1,0:T(4,128)}) async-done(((f32[4,1600]{1,0:T(4,128)}, f32[4,1600]{1,0:T(4,128)}, f32[4,1600]{1,0:T(4,128)}, f32[4,1600]{1,0:T(4,128)}), (f32[4,1600]{1,0:T(4,128)}, f32[4,1600]{1,0:T(4,128)}, f32[4,1600]{1,0:T(4,128)}, f32[4,1600]{1,0:T(4,128)})) %all-reduce.9.cloned.1.call-update) | async-done | bytes 102416 | tf_op jit(solution)/shard_map/psum | solution.py:75
  332.0 1.0 fusion.208
  333.0 0.2 multiply_reduce_fusion
  333.2 0.2 multiply_reduce_fusion.1
  333.5 3.9 fusion.83
  337.4 3.9 fusion.74
  341.3 0.2 multiply_reduce_fusion.2
  341.5 3.9 fusion.65
  345.4 0.2 multiply_reduce_fusion.3
  345.6 3.9 fusion.56
  349.6 2.3 copy.26
  351.8 2.3 copy.27
  354.1 66.6 %all-reduce.7.cloned.1.call-done = (f32[4,1600]{1,0:T(4,128)}, f32[4,1600]{1,0:T(4,128)}, f32[4,1600]{1,0:T(4,128)}, f32[4,1600]{1,0:T(4,128)}) async-done(((f32[4,1600]{1,0:T(4,128)}, f32[4,1600]{1,0:T(4,128)}, f32[4,1600]{1,0:T(4,128)}, f32[4,1600]{1,0:T(4,128)}), (f32[4,1600]{1,0:T(4,128)}, f32[4,1600]{1,0:T(4,128)}, f32[4,1600]{1,0:T(4,128)}, f32[4,1600]{1,0:T(4,128)})) %all-reduce.7.cloned.1.call-update) | async-done | bytes 102416 | tf_op jit(solution)/shard_map/psum | solution.py:84
  420.7 0.8 fusion.84
  421.5 0.7 pad_maximum_fusion
  (79 shorter events, 1.8 us)
Async XLA Ops:
  7.2 326.2 %copy-start = (bf16[800,1600]{1,0:T(8,128)(2,1)S(1)}, bf16[800,1600]{1,0:T(8,128)(2,1)}, u32[]{:S(2)}) copy-start(bf16[800,1600]{1,0:T(8,128)(2,1)} %param.28) | copy-start | bytes 7680004
  7.2 5.3 %copy-start.5 = (bf16[4,4,1600]{2,1,0:T(4,128)(2,1)S(1)}, bf16[4,4,1600]{2,1,0:T(4,128)(2,1)}, u32[]{:S(2)}) copy-start(bf16[4,4,1600]{2,1,0:T(4,128)(2,1)} %param.17) | copy-start | bytes 153604
  7.2 5.3 %copy-start.6 = (f32[1600]{0:T(1024)S(1)}, f32[1600]{0:T(1024)}, u32[]{:S(2)}) copy-start(f32[1600]{0:T(1024)} %param.19) | copy-start | bytes 19204
  7.2 5.3 %copy-start.7 = (f32[1600]{0:T(1024)S(1)}, f32[1600]{0:T(1024)}, u32[]{:S(2)}) copy-start(f32[1600]{0:T(1024)} %param.18) | copy-start | bytes 19204
  7.2 5.3 %copy-start.10 = (f32[3,256]{1,0:T(4,128)S(1)}, f32[3,256]{1,0:T(4,128)}, u32[]{:S(2)}) copy-start(f32[3,256]{1,0:T(4,128)} %param.21) | copy-start | bytes 9220
  7.2 324.8 %all-reduce.9.cloned.1.call-start = ((), (), s32[]{:S(2)}) async-start(), calls=%async_computation.1 | async-start | bytes 212992 | tf_op jit(solution)/shard_map/psum | solution.py:75
  8.2 4.4 %copy-start.1 = (bf16[1600,3,256]{2,0,1:T(8,128)(2,1)S(1)}, bf16[1600,3,256]{2,0,1:T(8,128)(2,1)}, u32[]{:S(2)}) copy-start(bf16[1600,3,256]{2,0,1:T(8,128)(2,1)} %param.20) | copy-start | bytes 7372804
  15.8 4.6 %copy-start.17 = (s32[4,32]{1,0:T(4,128)S(1)}, s32[4,32]{1,0:T(4,128)}, u32[]{:S(2)}) copy-start(s32[4,32]{1,0:T(4,128)} %param.32) | copy-start | bytes 1540
  15.8 4.7 %copy-start.16 = (s32[4,4]{1,0:T(4,128)S(1)}, s32[4,4]{1,0:T(4,128)}, u32[]{:S(2)}) copy-start(s32[4,4]{1,0:T(4,128)} %param.33) | copy-start | bytes 196
  25.7 1.0 copy-start.3
  28.2 8.7 %copy-start.4 = (bf16[4,512,256]{1,2,0:T(8,128)(2,1)S(1)}, bf16[4,512,256]{1,2,0:T(8,128)(2,1)}, u32[]{:S(2)}) copy-start(bf16[4,512,256]{1,2,0:T(8,128)(2,1)} %get-tuple-element.73) | copy-start | bytes 3145732
  28.2 8.7 %copy-start.14 = (bf16[4,4,512,1]{2,1,0,3:T(4,128)(2,1)S(1)}, bf16[4,4,512,1]{2,1,0,3:T(4,128)(2,1)}, u32[]{:S(2)}) copy-start(bf16[4,4,512,1]{2,1,0,3:T(4,128)(2,1)} %get-tuple-element.68) | copy-start | bytes 49156
  32.7 79.5 %copy-start.13 = (f32[4,4]{1,0:T(4,128)}, f32[4,4]{1,0:T(4,128)S(1)}, u32[]{:S(2)}) copy-start(f32[4,4]{1,0:T(4,128)S(1)} %select_reduce_fusion.2) | copy-start | bytes 196
  35.5 219.3 %copy-start.2 = (bf16[256,1600]{0,1:T(8,128)(2,1)S(1)}, bf16[256,1600]{0,1:T(8,128)(2,1)}, u32[]{:S(2)}) copy-start(bf16[256,1600]{0,1:T(8,128)(2,1)} %param.22) | copy-start | bytes 2457604
  35.6 76.6 %copy-start.12 = (f32[4,4]{1,0:T(4,128)}, f32[4,4]{1,0:T(4,128)S(1)}, u32[]{:S(2)}) copy-start(f32[4,4]{1,0:T(4,128)S(1)} %select_reduce_fusion.3) | copy-start | bytes 196
  113.8 219.6 %copy-start.8 = (f32[1600]{0:T(1024)S(1)}, f32[1600]{0:T(1024)}, u32[]{:S(2)}) copy-start(f32[1600]{0:T(1024)} %param.25) | copy-start | bytes 19204
  113.8 219.6 %copy-start.9 = (f32[1600]{0:T(1024)S(1)}, f32[1600]{0:T(1024)}, u32[]{:S(2)}) copy-start(f32[1600]{0:T(1024)} %param.24) | copy-start | bytes 19204
  113.8 219.6 %copy-start.11 = (f32[800]{0:T(1024)S(1)}, f32[800]{0:T(1024)}, u32[]{:S(2)}) copy-start(f32[800]{0:T(1024)} %param.27) | copy-start | bytes 9604
  261.3 159.4 %all-reduce.7.cloned.1.call-start = ((), (), s32[]{:S(2)}) async-start(), calls=%async_computation | async-start | bytes 212992 | tf_op jit(solution)/shard_map/psum | solution.py:84
  349.6 71.2 %copy-start.15 = (f32[1600]{0:T(1024)S(1)}, f32[1600]{0:T(1024)}, u32[]{:S(2)}) copy-start(f32[1600]{0:T(1024)} %param.29) | copy-start | bytes 19204
Sparse Core Ops, SparseCore 0:
  261.4 70.5 all-reduce.8
  349.7 70.9 all-reduce.6
where the time goes:
time: 435 us; the launch traced here: 429 us
  blocking collectives  188 us (43%)
  waiting for transfers between devices  137 us (31%)
  matrix products  38 us (9%)
  local copies, waits for them, and re-layouts  26.2 us (6%)
  other arithmetic  24.7 us (6%)
  between operations  14.3 us (3%)
    psum x1, blocking collectives, merge_heads(): lax.psum((totals * factor, blended * widen_heads(factor)), 'seq')  122 us
    psum x1, waiting for transfers between devices, finish(): lax.psum(jnp.dot(attended, output_weight, preferred_element_type=jnp.floa...  70.7 us
    pmax x1, blocking collectives, merge_heads(): highest = lax.pmax(peaks, 'seq')  66.8 us
    psum x1, waiting for transfers between devices, finish(): lax.psum(jnp.dot(hidden, contract_weight, preferred_element_type=jnp.floa...  66.6 us
    dot_general x4, matrix products, finish(): jnp.dot(hidden, contract_weight, preferred_element_type=jnp.float32)  15.7 us
    broadcast_in_dim x8, local copies, waits for them, and re-layouts, widen_heads(): return jnp.repeat(per_head, HEAD_DIM, axis=-1)  10.9 us
    unnamed x40, local copies, waits for them, and re-layouts  10.2 us
  transfers between devices with their start and end apart: 2, of which 2 were waited for; matrix products, arithmetic and copies ran while one was open for 1% of the time, Pallas kernels for 0%

commit v1 on v0

v1 whole, which is shorter than its diff:
```python
import functools
import math

import jax
import jax.numpy as jnp
from jax import lax
from jax.experimental import pallas as pl
from jax.experimental.pallas import tpu as pltpu
from jax.sharding import PartitionSpec as P

HEAD_DIM = 64
MESH = pl.DeviceIdType.MESH
NEG = -1e30
F32 = jnp.float32
BF16 = jnp.bfloat16


def layer_norm(values, gain, shift):
    center = values - jnp.mean(values, axis=-1, keepdims=True)
    spread = jnp.mean(center * center, axis=-1, keepdims=True)
    return center * lax.rsqrt(spread + 1e-05) * gain + shift


def as_row(ref):
    return ref[...].reshape(1, ref.shape[0])


def dot_nt(a, b):
    return lax.dot_general(a, b, (((1,), (1,)), ((), ())), preferred_element_type=F32)


def layer_kernel(
    cfg,
    tok_h,
    g1_h,
    s1_h,
    win_h,
    bin_h,
    wout_h,
    bout_h,
    g2_h,
    s2_h,
    wexp_h,
    bexp_h,
    wcon_h,
    bcon_h,
    key_h,
    val_h,
    fill_h,
    own_h,
    hid_o,
    nk_o,
    nv_o,
    tok_v,
    g1_v,
    s1_v,
    win_v,
    bin_v,
    wout_v,
    bout_v,
    g2_v,
    s2_v,
    wexp_v,
    bexp_v,
    wcon_v,
    bcon_v,
    key_v,
    val_v,
    fill_s,
    own_s,
    x_v,
    kn_v,
    vn_v,
    mid_v,
    sbuf,
    rbuf,
    p2buf,
    r2buf,
    p3buf,
    r3buf,
    fbuf,
    obuf,
    load_sem,
    store_sem,
    send_sem,
    recv_sem,
):
    side, planes, steps, requests, slots, width, model, units = cfg
    chips = side * side
    shards = 2 * chips
    rows = steps * requests
    heads = width // HEAD_DIM
    cut_d = (model // 2) // 128 * 128
    win_d = model - cut_d
    pad_d = -(-win_d // 128) * 128
    cut_f = (units // 2) // 128 * 128
    win_f = units - cut_f

    shard = lax.axis_index("seq")
    z = lax.axis_index("tensor")
    chip = shard // 2
    core = shard % 2
    cx = chip // side
    cy = chip % side

    load_count = [0]

    def load(src, dst):
        copy = pltpu.make_async_copy(src, dst, load_sem.at[load_count[0]])
        load_count[0] += 1
        copy.start()
        return copy

    c_small = [load(tok_h, tok_v), load(g1_h, g1_v), load(s1_h, s1_v)]
    c_win = [load(win_h.at[0], win_v.at[0])]
    c_bin = load(bin_h, bin_v)
    c_fill = [load(fill_h, fill_s), load(own_h, own_s)]
    c_win += [load(win_h.at[1], win_v.at[1])]
    c_key = [load(key_h.at[b], key_v.at[b]) for b in range(requests)]
    c_win += [load(win_h.at[2], win_v.at[2])]
    c_val = [load(val_h.at[b], val_v.at[b]) for b in range(requests)]
    c_late = [load(bout_h, bout_v), load(g2_h, g2_v), load(s2_h, s2_v)]
    c_late += [load(bexp_h, bexp_v), load(bcon_h, bcon_v)]
    row_d = pl.multiple_of(core * cut_d, 128)
    row_f = pl.multiple_of(core * cut_f, 128)
    c_wout = load(wout_h.at[pl.ds(row_d, win_d)], wout_v)
    c_wexp = load(wexp_h.at[pl.ds(row_f, win_f)], wexp_v)
    c_wcon = load(wcon_h.at[pl.ds(row_f, win_f)], wcon_v)

    offsets = sorted(
        ((dx, dy) for dx in range(side) for dy in range(side)),
        key=lambda o: -(min(o[0], side - o[0]) + min(o[1], side - o[1])),
    )
    plane_peers = []
    for dx, dy in offsets:
        other = lax.rem(cx + dx, side) * side + lax.rem(cy + dy, side)
        if dx == 0 and dy == 0:
            plane_peers.append((other, 1 - core))
        else:
            plane_peers.append((other, 0))
            plane_peers.append((other, 1))
    z_offsets = sorted(range(planes), key=lambda d: -min(d, planes - d))
    column_peers = []
    for dz in z_offsets:
        other = lax.rem(z + dz, planes)
        if dz == 0:
            column_peers.append((other, None))
        else:
            column_peers.append((other, 0))
            column_peers.append((other, 1))

    barrier = pltpu.get_barrier_semaphore()
    signals = 0
    for other, k in plane_peers:
        pl.semaphore_signal(barrier, inc=1, device_id=(other * 2 + k, z), device_id_type=MESH)
        signals += 1
    for other, k in column_peers:
        if k is not None:
            pl.semaphore_signal(
                barrier, inc=1, device_id=(chip * 2 + k, other), device_id_type=MESH
            )
            signals += 1

    for c in c_small:
        c.wait()
    for t in range(steps):
        x_v[pl.ds(t * requests, requests), :] = tok_v[t].astype(F32)
    normed = layer_norm(x_v[...], as_row(g1_v), as_row(s1_v)).astype(BF16)
    c_bin.wait()
    packed = []
    for part in range(3):
        c_win[part].wait()
        packed.append(
            (
                jnp.dot(normed, win_v[part], preferred_element_type=F32)
                + bin_v[part : part + 1, :]
            ).astype(BF16)
        )
    query, key_new, value_new = packed
    kn_v[...] = key_new.astype(F32)
    vn_v[...] = value_new.astype(F32)

    for c in c_fill:
        c.wait()
    fills = [fill_s[b, shard] for b in range(requests)]
    owned = [[(own_s[t, b] == shard).astype(jnp.int32) for b in range(requests)] for t in range(steps)]
    places = []
    for b in range(requests):
        at = fills[b]
        row = []
        for t in range(steps):
            row.append(jnp.where(owned[t][b] > 0, at, -1))
            at = at + owned[t][b]
        places.append(row)

    total_rows = heads * rows
    row_id = lax.broadcasted_iota(jnp.int32, (total_rows, 1), 0)
    row_b = row_id % requests
    row_t = (row_id // requests) % steps
    fill_col = jnp.zeros((total_rows, 1), jnp.int32)
    for b in range(requests):
        fill_col = jnp.where(row_b == b, fills[b], fill_col)
    col = lax.broadcasted_iota(jnp.int32, (1, rows), 1)
    own_row = jnp.zeros((1, rows), jnp.int32)
    for t in range(steps):
        for b in range(requests):
            own_row = jnp.where(col == t * requests + b, owned[t][b], own_row)
    new_ok = (
        (col % requests == row_b) & (col // requests <= row_t) & (own_row > 0)
    )

    lane_head = lax.broadcasted_iota(jnp.int32, (rows, width), 1) // HEAD_DIM
    query_f = query.astype(F32)
    query_heads = jnp.concatenate(
        [jnp.where(lane_head == h, query_f, 0.0) for h in range(heads)], axis=0
    ).astype(BF16)
    scale = 1.0 / math.sqrt(HEAD_DIM)
    scores_new = jnp.where(new_ok, dot_nt(query_heads, key_new) * scale, NEG)
    scores = None
    for b in range(requests):
        c_key[b].wait()
        part = dot_nt(query_heads, key_v[b])
        scores = part if scores is None else jnp.where(row_b == b, part, scores)
    slot = lax.broadcasted_iota(jnp.int32, (total_rows, slots), 1)
    usable = slot < fill_col
    scores = jnp.where(usable, scores * scale, NEG)
    peaks = jnp.maximum(
        jnp.max(scores, axis=-1, keepdims=True), jnp.max(scores_new, axis=-1, keepdims=True)
    )
    weights = jnp.where(usable, jnp.exp(scores - peaks), 0.0)
    weights_new = jnp.where(new_ok, jnp.exp(scores_new - peaks), 0.0)
    totals = jnp.sum(weights, axis=-1, keepdims=True) + jnp.sum(
        weights_new, axis=-1, keepdims=True
    )
    blended = jnp.dot(weights_new.astype(BF16), value_new, preferred_element_type=F32)
    for b in range(requests):
        c_val[b].wait()
        blended = blended + jnp.dot(
            jnp.where(row_b == b, weights, 0.0).astype(BF16),
            val_v[b],
            preferred_element_type=F32,
        )
    lane = lax.broadcasted_iota(jnp.int32, (rows, 128), 1)
    merged = jnp.zeros((rows, width), F32)
    stats = jnp.zeros((rows, 128), F32)
    for h in range(heads):
        block = slice(h * rows, (h + 1) * rows)
        merged = jnp.where(lane_head == h, blended[block], merged)
        stats = jnp.where(lane == h, peaks[block], stats)
        stats = jnp.where(lane == heads + h, totals[block], stats)
    sbuf[:, 0, 0:width] = merged
    sbuf[:, 0, width : width + 128] = stats

    pl.semaphore_wait(barrier, signals)
    for other, k in plane_peers:
        pltpu.make_async_remote_copy(
            src_ref=sbuf.at[other],
            dst_ref=rbuf.at[shard],
            send_sem=send_sem.at[0],
            recv_sem=recv_sem.at[0],
            device_id=(other * 2 + k, z),
            device_id_type=MESH,
        ).start()
    rbuf[shard] = sbuf[chip]

    stores = []
    chunk = min(64, slots)
    for b in range(requests):

        def update(i, carry, b=b):
            start = pl.multiple_of(i * chunk, chunk)
            slot_id = start + lax.broadcasted_iota(jnp.int32, (chunk, 1), 0)
            for new, cache in ((kn_v, key_v), (vn_v, val_v)):
                block = cache[b, pl.ds(start, chunk), :].astype(F32)
                for t in range(steps):
                    r = t * requests + b
                    block = jnp.where(slot_id == places[b][t], new[r : r + 1, :], block)
                cache[b, pl.ds(start, chunk), :] = block.astype(BF16)
            return carry

        lax.fori_loop(0, slots // chunk, update, 0)
        for i, (cache, out) in enumerate(((key_v, nk_o), (val_v, nv_o))):
            copy = pltpu.make_async_copy(cache.at[b], out.at[b], store_sem.at[2 * b + i])
            copy.start()
            stores.append(copy)

    for c in c_late:
        c.wait()
    c_wout.wait()

    def wait_all(buf, count, sem):
        pltpu.make_async_copy(buf.at[pl.ds(0, count)], buf.at[pl.ds(0, count)], sem).wait()

    wait_all(rbuf, shards - 1, recv_sem.at[0])
    got = rbuf[:, 0, :]
    got_stats = got[:, width : width + 128]
    highest = jnp.max(got_stats, axis=0, keepdims=True)
    factor = jnp.exp(got_stats - highest)
    factor_at = pltpu.roll(factor, heads, 1)
    sums = jnp.sum(factor_at * got_stats, axis=0, keepdims=True)
    wide_head = lax.broadcasted_iota(jnp.int32, (shards, width), 1) // HEAD_DIM
    row_head = lax.broadcasted_iota(jnp.int32, (1, width), 1) // HEAD_DIM
    wide = jnp.zeros((shards, width), F32)
    below = jnp.ones((1, width), F32)
    for h in range(heads):
        wide = jnp.where(wide_head == h, factor[:, h : h + 1], wide)
        below = jnp.where(row_head == h, sums[:, heads + h : heads + h + 1], below)
    attended = jnp.sum(got[:, 0:width] * wide, axis=0, keepdims=True) / below
    attended = jnp.broadcast_to(attended, (16, width)).astype(BF16)

    slot_z = core * planes + z
    part = dot_nt(attended, wout_v[...])[0:1, :]
    part = jnp.concatenate([part, jnp.zeros((1, pad_d - win_d), F32)], axis=1)
    p2buf[0] = part
    r2buf[slot_z] = part
    for other, k in column_peers:
        pltpu.make_async_remote_copy(
            src_ref=p2buf.at[0],
            dst_ref=r2buf.at[slot_z],
            send_sem=send_sem.at[1],
            recv_sem=recv_sem.at[1],
            device_id=(chip * 2 + (1 - core if k is None else k), other),
            device_id_type=MESH,
        ).start()
    row_x = x_v[pl.ds(chip, 1), :] + as_row(bout_v)
    c_wexp.wait()
    c_wcon.wait()
    wait_all(r2buf, 2 * planes - 1, recv_sem.at[1])
    low = jnp.sum(r2buf[0:planes, 0, :], axis=0, keepdims=True)
    high = jnp.sum(r2buf[planes : 2 * planes, 0, :], axis=0, keepdims=True)
    middle = row_x + jnp.concatenate([low[:, :cut_d], high[:, :win_d]], axis=1)
    mid_v[:, 0:model] = middle + as_row(bcon_v)
    mid_v[:, model:] = jnp.zeros((1, mid_v.shape[1] - model), F32)

    second = layer_norm(middle, as_row(g2_v), as_row(s2_v))
    second = jnp.broadcast_to(second, (16, model)).astype(BF16)
    bias = as_row(bexp_v)
    bias = jnp.where(core == 0, bias[:, 0:win_f], bias[:, cut_f:units])
    hidden = jax.nn.gelu(dot_nt(second, wexp_v[...]) + bias, approximate=True)
    unit = lax.broadcasted_iota(jnp.int32, (16, win_f), 1)
    hidden = jnp.where(unit < jnp.where(core == 0, cut_f, win_f), hidden, 0.0).astype(BF16)
    part = jnp.dot(hidden, wcon_v[...], preferred_element_type=F32)[0:1, :]
    p3buf[:, 0:model] = part
    p3buf[:, model:] = jnp.zeros((1, p3buf.shape[1] - model), F32)

    for other, k in column_peers:
        to = 1 - core if k is None else k
        lanes = pl.ds(pl.multiple_of(to * cut_d, 128), pad_d)
        pltpu.make_async_remote_copy(
            src_ref=p3buf.at[:, lanes],
            dst_ref=r3buf.at[slot_z],
            send_sem=send_sem.at[2],
            recv_sem=recv_sem.at[2],
            device_id=(chip * 2 + to, other),
            device_id_type=MESH,
        ).start()
    own_lanes = pl.ds(row_d, pad_d)
    r3buf[slot_z] = p3buf[:, own_lanes]
    wait_all(r3buf, 2 * planes - 1, recv_sem.at[2])
    result = jnp.sum(r3buf[:, 0, :], axis=0, keepdims=True) + mid_v[:, own_lanes]
    slot_o = core * chips + chip
    fbuf[0] = result
    obuf[slot_o] = result

    for other, k in plane_peers:
        pltpu.make_async_remote_copy(
            src_ref=fbuf.at[0],
            dst_ref=obuf.at[slot_o],
            send_sem=send_sem.at[3],
            recv_sem=recv_sem.at[3],
            device_id=(other * 2 + k, z),
            device_id_type=MESH,
        ).start()
    for c in stores:
        c.wait()
    wait_all(rbuf, shards - 1, send_sem.at[0])
    wait_all(r2buf, 2 * planes - 1, send_sem.at[1])
    wait_all(r3buf, 2 * planes - 1, send_sem.at[2])
    wait_all(obuf, shards - 1, recv_sem.at[3])
    hid_o[:, 0:cut_d] = obuf[0:chips, 0, 0:cut_d].astype(BF16)
    hid_o[:, cut_d:model] = obuf[chips : 2 * chips, 0, 0:win_d].astype(BF16)
    wait_all(obuf, shards - 1, send_sem.at[3])


def per_device(
    side,
    planes,
    tokens,
    first_gain,
    first_shift,
    input_weight,
    input_bias,
    output_weight,
    output_bias,
    second_gain,
    second_shift,
    expand_weight,
    expand_bias,
    contract_weight,
    contract_bias,
    key_cache,
    value_cache,
    cache_fill,
    owner_shard,
):
    steps, requests, model = tokens.shape
    width = input_weight.shape[2]
    units = expand_weight.shape[1]
    slots = key_cache.shape[1]
    rows = steps * requests
    chips = side * side
    shards = 2 * chips
    cut_d = (model // 2) // 128 * 128
    win_d = model - cut_d
    pad_d = -(-win_d // 128) * 128
    win_f = units - (units // 2) // 128 * 128
    cfg = (side, planes, steps, requests, slots, width, model, units)
    args = (
        tokens,
        first_gain,
        first_shift,
        input_weight.transpose(1, 0, 2),
        input_bias,
        output_weight.T,
        output_bias,
        second_gain,
        second_shift,
        expand_weight.T,
        expand_bias,
        contract_weight,
        contract_bias,
        key_cache,
        value_cache,
        cache_fill,
        owner_shard,
    )
    row = pltpu.VMEM((model,), F32)
    hidden, new_keys, new_values = pl.pallas_call(
        functools.partial(layer_kernel, cfg),
        out_shape=(
            jax.ShapeDtypeStruct((rows, model), BF16),
            jax.ShapeDtypeStruct(key_cache.shape, BF16),
            jax.ShapeDtypeStruct(value_cache.shape, BF16),
        ),
        in_specs=[pl.BlockSpec(memory_space=pl.ANY)] * len(args),
        out_specs=(
            pl.BlockSpec(memory_space=pltpu.VMEM),
            pl.BlockSpec(memory_space=pl.ANY),
            pl.BlockSpec(memory_space=pl.ANY),
        ),
        scratch_shapes=[
            pltpu.VMEM(tokens.shape, BF16),
            row,
            row,
            pltpu.VMEM((3, model, width), BF16),
            pltpu.VMEM((3, width), F32),
            pltpu.VMEM((win_d, width), BF16),
            row,
            row,
            row,
            pltpu.VMEM((win_f, model), BF16),
            pltpu.VMEM((units,), F32),
            pltpu.VMEM((win_f, model), BF16),
            row,
            pltpu.VMEM(key_cache.shape, BF16),
            pltpu.VMEM(value_cache.shape, BF16),
            pltpu.SMEM(cache_fill.shape, jnp.int32),
            pltpu.SMEM(owner_shard.shape, jnp.int32),
            pltpu.VMEM((rows, model), F32),
            pltpu.VMEM((rows, width), F32),
            pltpu.VMEM((rows, width), F32),
            pltpu.VMEM((1, cut_d + pad_d), F32),
            pltpu.VMEM((rows, 1, width + 128), F32),
            pltpu.VMEM((shards, 1, width + 128), F32),
            pltpu.VMEM((1, 1, pad_d), F32),
            pltpu.VMEM((2 * planes, 1, pad_d), F32),
            pltpu.VMEM((1, cut_d + pad_d), F32),
            pltpu.VMEM((2 * planes, 1, pad_d), F32),
            pltpu.VMEM((1, 1, pad_d), F32),
            pltpu.VMEM((shards, 1, pad_d), F32),
            pltpu.SemaphoreType.DMA((17 + 2 + 2 * (requests - 1),)),
            pltpu.SemaphoreType.DMA((2 * requests,)),
            pltpu.SemaphoreType.DMA((4,)),
            pltpu.SemaphoreType.DMA((4,)),
        ],
        compiler_params=pltpu.CompilerParams(collective_id=0, has_side_effects=True),
        name="layer",
    )(*args)
    return (hidden.reshape(steps, requests, model), new_keys, new_values)


def solution(mesh):
    side = math.isqrt(mesh.shape["seq"] // 2)
    return jax.shard_map(
        functools.partial(per_device, side, mesh.shape["tensor"]),
        mesh=mesh,
        in_specs=(
            P(),
            P(),
            P(),
            P(None, None, "tensor"),
            P(None, "tensor"),
            P("tensor", None),
            P(),
            P(),
            P(),
            P(None, "tensor"),
            P("tensor"),
            P("tensor", None),
            P(),
            P(None, "seq", "tensor"),
            P(None, "seq", "tensor"),
            P(),
            P(),
        ),
        out_specs=(P(), P(None, "seq", "tensor"), P(None, "seq", "tensor")),
        check_vma=False,
    )
```

time: 435 us -> 37 us (0.09); the launches traced: 429 us -> 36.9 us
  blocking collectives: 188 us -> 0 us
  waiting for transfers between devices: 137 us -> 0 us
  matrix products: 38 us -> 0 us
  Pallas kernels: 0 us -> 31.5 us
  other arithmetic: 24.7 us -> 0 us
  local copies, waits for them, and re-layouts: 26.2 us -> 4.77 us
  between operations: 14.3 us -> 0.66 us
    psum x2 -> x0, waiting for transfers between devices: 137 us -> none  [the longest x1 70.7 us: finish(): lax.psum(jnp.dot(attended, output_weight, preferred_element_type=jnp.floa...]
    psum x1 -> x0, blocking collectives: 122 us -> none  [merge_heads(): lax.psum((totals * factor, blended * widen_heads(factor)), 'seq')]
    pmax x1 -> x0, blocking collectives: 66.8 us -> none  [merge_heads(): highest = lax.pmax(peaks, 'seq')]
    dot_general x20 -> x0, matrix products: 38 us -> none  [the longest x4 15.7 us: finish(): jnp.dot(hidden, contract_weight, preferred_element_type=jnp.float32)]
    pallas_call x0 -> x1, Pallas kernels: none -> 31.5 us  [per_device(): pl.pallas_call(functools.partial(layer_kernel, cfg), out_shape=(jax.Shape...]
    broadcast_in_dim x8 -> x0, local copies, waits for them, and re-layouts: 10.9 us -> none  [widen_heads(): return jnp.repeat(per_head, HEAD_DIM, axis=-1)]
    reduce_sum x12 -> x0, other arithmetic: 8.48 us -> none  [the longest x4 4.51 us: attend(): totals = jnp.sum(weights, axis=-1)]
    unnamed x40 -> x4, local copies, waits for them, and re-layouts: 10.2 us -> 3.24 us
  transfers between devices with their start and end apart: 2 -> 0, of which waited for: 2 -> 0; matrix products, arithmetic and copies ran while one was open for 1% -> 0% of each run, Pallas kernels for 0% -> 0%
where the time goes in v1:
time: 37 us; the launch traced here: 36.9 us
  Pallas kernels  31.5 us (85%)
  local copies, waits for them, and re-layouts  4.77 us (13%)
  between operations  0.66 us (2%)
    pallas_call x1, Pallas kernels, per_device(): pl.pallas_call(functools.partial(layer_kernel, cfg), out_shape=(jax.Shape...  31.5 us
    unnamed x4, local copies, waits for them, and re-layouts  3.24 us
    reshape x1, local copies, waits for them, and re-layouts, per_device(): return (hidden.reshape(steps, requests, model), new_keys, new_values)  1.54 us

profile of v1, /device:TPU:1, one launch (start us, length us, event | category | flops | bytes accessed | tf_op | source)
XLA Modules:
  0.0 36.9 jit_solution(16518096874682161965)
XLA Ops:
  0.6 31.5 %layer.1 = (bf16[16,1600]{1,0:T(8,128)(2,1)}, bf16[4,512,256]{2,1,0:T(8,128)(2,1)}, bf16[4,512,256]{2,1,0:T(8,128)(2,1)}) custom-call(bf16[4,4,1600]{2,1,0:T(4,128)(2,1)} %tok_h.1, f32[1600]{0:T(1024)} %g1_h.1, f32[1600]{0:T(1024)} %s1_h.1, bf16[3,1600,256]{2,1,0:T(8,128)(2,1)} %bitcast.4, f32[3,256]{1,0:T(4,128)} %bin_h.1, bf16[1600,256]{1,0:T(8,128)(2,1)} %bitcast.5, ...), custom_call_target="tpu_custom_call" | custom-call | tf_op jit(solution)/shard_map/layer/pallas_call | solution.py:438
  32.1 0.0 copy-start
  32.1 1.5 %reshape.9 = bf16[4,4,1600]{2,1,0:T(4,128)(2,1)} reshape(bf16[16,1600]{1,0:T(8,128)(2,1)} %get-tuple-element.6) | data formatting | bytes 102400 | tf_op jit(solution)/shard_map/reshape | solution.py:489
  33.7 2.3 %copy.22 = bf16[4,512,256]{2,1,0:T(8,128)(2,1)} copy(bf16[4,512,256]{2,1,0:T(8,128)(2,1)} %get-tuple-element.13) | data formatting | bytes 2097152
  35.9 0.0 copy-done
  35.9 1.0 %copy.23 = bf16[4,512,256]{2,1,0:T(8,128)(2,1)} copy(bf16[4,512,256]{2,1,0:T(8,128)(2,1)S(1)} %copy-done) | data formatting | bytes 2097152
Async XLA Ops:
  32.1 3.8 %copy-start = (bf16[4,512,256]{2,1,0:T(8,128)(2,1)S(1)}, bf16[4,512,256]{2,1,0:T(8,128)(2,1)}, u32[]{:S(2)}) copy-start(bf16[4,512,256]{2,1,0:T(8,128)(2,1)} %get-tuple-element.14) | copy-start | bytes 3145732

commit v2 on v1

v2 whole, which is shorter than its diff:
```python
import contextlib
import functools
import math

import jax
import jax.numpy as jnp
from jax import lax
from jax.experimental import pallas as pl
from jax.experimental.pallas import tpu as pltpu
from jax.sharding import PartitionSpec as P

HEAD_DIM = 64
MESH = pl.DeviceIdType.MESH
NEG = -1e30
F32 = jnp.float32
BF16 = jnp.bfloat16


def layer_norm(values, gain, shift):
    center = values - jnp.mean(values, axis=-1, keepdims=True)
    spread = jnp.mean(center * center, axis=-1, keepdims=True)
    return center * lax.rsqrt(spread + 1e-05) * gain + shift


TRACE = False


def scope(name):
    return jax.named_scope(name) if TRACE else contextlib.nullcontext()


def as_row(ref):
    return ref[...].reshape(1, ref.shape[0])


def dot_nt(a, b):
    return lax.dot_general(a, b, (((1,), (1,)), ((), ())), preferred_element_type=F32)


def layer_kernel(
    cfg,
    tok_h,
    g1_h,
    s1_h,
    win_h,
    bin_h,
    wout_h,
    bout_h,
    g2_h,
    s2_h,
    wexp_h,
    bexp_h,
    wcon_h,
    bcon_h,
    key_h,
    val_h,
    fill_h,
    own_h,
    hid_o,
    key_v,
    val_v,
    tok_v,
    g1_v,
    s1_v,
    win_v,
    bin_v,
    wout_v,
    bout_v,
    g2_v,
    s2_v,
    wexp_v,
    bexp_v,
    wcon_v,
    bcon_v,
    fill_s,
    own_s,
    x_v,
    kn_v,
    vn_v,
    sbuf,
    rbuf,
    p2buf,
    r2buf,
    p3buf,
    r3buf,
    fbuf,
    obuf,
    load_sem,
    send_sem,
    recv_sem,
):
    side, planes, steps, requests, slots, width, model, units = cfg
    half = side // 2
    chips = side * side
    shards = 2 * chips
    rows = steps * requests
    heads = width // HEAD_DIM
    wide_d = p2buf.shape[-1]

    shard = lax.axis_index("seq")
    z = lax.axis_index("tensor")
    chip = shard // 2
    core = shard % 2
    cx = chip // side
    cy = chip % side

    def row_of(x, y, k):
        return 2 * (lax.rem(x, half) * side + lax.rem(y + half * (x // half), side)) + k

    my_row = row_of(cx, cy, core)

    load_count = [0]

    def load(src, dst):
        copy = pltpu.make_async_copy(src, dst, load_sem.at[load_count[0]])
        load_count[0] += 1
        copy.start()
        return copy

    with scope("issue"):
        c_small = [load(tok_h, tok_v), load(g1_h, g1_v), load(s1_h, s1_v)]
        c_win = [load(win_h.at[0], win_v.at[0])]
        c_bin = load(bin_h, bin_v)
        c_fill = [load(fill_h, fill_s), load(own_h, own_s)]
        c_key = [load(key_h.at[b], key_v.at[b]) for b in range(requests)]
        c_win += [load(win_h.at[1], win_v.at[1]), load(win_h.at[2], win_v.at[2])]
        c_val = [load(val_h.at[b], val_v.at[b]) for b in range(requests)]

    def distance(o):
        return min(o[0], side - o[0]) + min(o[1], side - o[1])

    offsets = sorted(
        ((dx, dy) for dx in range(side) for dy in range(side)), key=lambda o: -distance(o)
    )
    plane_peers = []
    for dx, dy in offsets:
        other = (lax.rem(cx + dx, side), lax.rem(cy + dy, side))
        if dx == 0 and dy == 0:
            plane_peers.append((*other, 1 - core))
        else:
            plane_peers.append((*other, 0))
            plane_peers.append((*other, 1))
    column_peers = [
        lax.rem(z + dz, planes)
        for dz in sorted(range(1, planes), key=lambda d: -min(d, planes - d))
    ]

    def seq_of(x, y, k):
        return (x * side + y) * 2 + k

    barrier = pltpu.get_barrier_semaphore()
    with scope("signals"):
        for peer in plane_peers:
            pl.semaphore_signal(
                barrier, inc=1, device_id=(seq_of(*peer), z), device_id_type=MESH
            )
        for other in column_peers:
            pl.semaphore_signal(barrier, inc=1, device_id=(shard, other), device_id_type=MESH)

    with scope("norm1"):
        for c in c_small:
            c.wait()
        for t in range(steps):
            x_v[pl.ds(t * requests, requests), :] = tok_v[t].astype(F32)
        normed = layer_norm(x_v[...], as_row(g1_v), as_row(s1_v)).astype(BF16)
        c_bin.wait()

    def project(part):
        c_win[part].wait()
        return (
            jnp.dot(normed, win_v[part], preferred_element_type=F32) + bin_v[part : part + 1, :]
        ).astype(BF16)

    with scope("query"):
        query = project(0)

    for c in c_fill:
        c.wait()
    fills = [fill_s[b, shard] for b in range(requests)]
    owned = [
        [(own_s[t, b] == shard).astype(jnp.int32) for b in range(requests)] for t in range(steps)
    ]
    places = []
    for b in range(requests):
        at = fills[b]
        row = []
        for t in range(steps):
            row.append(jnp.where(owned[t][b] > 0, at, -1))
            at = at + owned[t][b]
        places.append(row)

    total_rows = heads * rows
    row_id = lax.broadcasted_iota(jnp.int32, (total_rows, 1), 0)
    row_b = row_id % requests
    row_t = (row_id // requests) % steps
    fill_col = jnp.zeros((total_rows, 1), jnp.int32)
    for b in range(requests):
        fill_col = jnp.where(row_b == b, fills[b], fill_col)
    col = lax.broadcasted_iota(jnp.int32, (1, rows), 1)
    own_row = jnp.zeros((1, rows), jnp.int32)
    for t in range(steps):
        for b in range(requests):
            own_row = jnp.where(col == t * requests + b, owned[t][b], own_row)
    new_ok = (col % requests == row_b) & (col // requests <= row_t) & (own_row > 0)

    lane_head = lax.broadcasted_iota(jnp.int32, (rows, width), 1) // HEAD_DIM
    query_f = query.astype(F32)
    query_heads = jnp.concatenate(
        [jnp.where(lane_head == h, query_f, 0.0) for h in range(heads)], axis=0
    ).astype(BF16)
    scale = 1.0 / math.sqrt(HEAD_DIM)
    scores = None
    with scope("scores"):
        for b in range(requests):
            c_key[b].wait()
            part = dot_nt(query_heads, key_v[b])
            scores = part if scores is None else jnp.where(row_b == b, part, scores)
    with scope("keyvalue"):
        key_new = project(1)
        value_new = project(2)
        kn_v[...] = key_new.astype(F32)
        vn_v[...] = value_new.astype(F32)
    with scope("attend"):
        scores_new = jnp.where(new_ok, dot_nt(query_heads, key_new) * scale, NEG)
        slot = lax.broadcasted_iota(jnp.int32, (total_rows, slots), 1)
        usable = slot < fill_col
        scores = jnp.where(usable, scores * scale, NEG)
        peaks = jnp.maximum(
            jnp.max(scores, axis=-1, keepdims=True), jnp.max(scores_new, axis=-1, keepdims=True)
        )
        weights = jnp.where(usable, jnp.exp(scores - peaks), 0.0)
        weights_new = jnp.where(new_ok, jnp.exp(scores_new - peaks), 0.0)
        totals = jnp.sum(weights, axis=-1, keepdims=True) + jnp.sum(
            weights_new, axis=-1, keepdims=True
        )
        blended = jnp.dot(weights_new.astype(BF16), value_new, preferred_element_type=F32)
        for b in range(requests):
            c_val[b].wait()
            blended = blended + jnp.dot(
                jnp.where(row_b == b, weights, 0.0).astype(BF16),
                val_v[b],
                preferred_element_type=F32,
            )
        lane = lax.broadcasted_iota(jnp.int32, (rows, 128), 1)
        merged = jnp.zeros((rows, width), F32)
        stats = jnp.zeros((rows, 128), F32)
        for h in range(heads):
            block = slice(h * rows, (h + 1) * rows)
            merged = jnp.where(lane_head == h, blended[block], merged)
            stats = jnp.where(lane == h, peaks[block], stats)
            stats = jnp.where(lane == heads + h, totals[block], stats)
        sbuf[:, 0, 0:width] = merged
        sbuf[:, 0, width : width + 128] = stats

    with scope("barrier"):
        pl.semaphore_wait(barrier, len(plane_peers) + len(column_peers))
    with scope("send1"):
        for peer in plane_peers:
            pltpu.make_async_remote_copy(
                src_ref=sbuf.at[row_of(*peer)],
                dst_ref=rbuf.at[shard],
                send_sem=send_sem.at[0],
                recv_sem=recv_sem.at[0],
                device_id=(seq_of(*peer), z),
                device_id_type=MESH,
            ).start()
        rbuf[shard] = sbuf[my_row]
        c_wout = load(wout_h, wout_v)
        c_late = [load(bout_h, bout_v), load(g2_h, g2_v), load(s2_h, s2_v)]
        c_late += [load(bexp_h, bexp_v), load(bcon_h, bcon_v)]
        c_wexp = load(wexp_h, wexp_v)
        c_wcon = load(wcon_h, wcon_v)

    with scope("caches"):
        chunk = min(64, slots)
        for b in range(requests):

            def update(i, carry, b=b):
                start = pl.multiple_of(i * chunk, chunk)
                slot_id = start + lax.broadcasted_iota(jnp.int32, (chunk, 1), 0)
                for new, cache in ((kn_v, key_v), (vn_v, val_v)):
                    block = cache[b, pl.ds(start, chunk), :].astype(F32)
                    for t in range(steps):
                        r = t * requests + b
                        block = jnp.where(slot_id == places[b][t], new[r : r + 1, :], block)
                    cache[b, pl.ds(start, chunk), :] = block.astype(BF16)
                return carry

            lax.fori_loop(0, slots // chunk, update, 0)

    with scope("wlate"):
        for c in c_late:
            c.wait()
        c_wout.wait()

    def wait_all(buf, count, sem):
        pltpu.make_async_copy(buf.at[pl.ds(0, count)], buf.at[pl.ds(0, count)], sem).wait()

    with scope("wait1"):
        wait_all(rbuf, shards - 1, recv_sem.at[0])
    with scope("project"):
        got = rbuf[:, 0, :]
        got_stats = got[:, width : width + 128]
        highest = jnp.max(got_stats, axis=0, keepdims=True)
        factor = jnp.exp(got_stats - highest)
        factor_at = pltpu.roll(factor, heads, 1)
        sums = jnp.sum(factor_at * got_stats, axis=0, keepdims=True)
        wide_head = lax.broadcasted_iota(jnp.int32, (shards, width), 1) // HEAD_DIM
        row_head = lax.broadcasted_iota(jnp.int32, (1, width), 1) // HEAD_DIM
        wide = jnp.zeros((shards, width), F32)
        below = jnp.ones((1, width), F32)
        for h in range(heads):
            wide = jnp.where(wide_head == h, factor[:, h : h + 1], wide)
            below = jnp.where(row_head == h, sums[:, heads + h : heads + h + 1], below)
        attended = jnp.sum(got[:, 0:width] * wide, axis=0, keepdims=True) / below
        attended = jnp.broadcast_to(attended, (16, width)).astype(BF16)
        part = dot_nt(attended, wout_v[...])[0:1, :]
        part = jnp.concatenate([part, jnp.zeros((1, wide_d - model), F32)], axis=1)

    def exchange(part, out, into, n):
        out[0] = part
        into[z] = part
        for other in column_peers:
            pltpu.make_async_remote_copy(
                src_ref=out.at[0],
                dst_ref=into.at[z],
                send_sem=send_sem.at[n],
                recv_sem=recv_sem.at[n],
                device_id=(shard, other),
                device_id_type=MESH,
            ).start()

    def collect(into, n):
        wait_all(into, planes - 1, recv_sem.at[n])
        return jnp.sum(into[:, 0, :], axis=0, keepdims=True)

    with scope("send2"):
        exchange(part, p2buf, r2buf, 1)
        row_x = x_v[pl.ds(my_row, 1), :] + as_row(bout_v)
        c_wexp.wait()
        c_wcon.wait()
    with scope("wait2"):
        heads_sum = collect(r2buf, 1)
    with scope("ffn"):
        middle = row_x + heads_sum[:, 0:model]
        second = layer_norm(middle, as_row(g2_v), as_row(s2_v))
        second = jnp.broadcast_to(second, (16, model)).astype(BF16)
        hidden = jax.nn.gelu(dot_nt(second, wexp_v[...]) + as_row(bexp_v), approximate=True)
        part = jnp.dot(hidden.astype(BF16), wcon_v[...], preferred_element_type=F32)[0:1, :]
        part = jnp.concatenate([part, jnp.zeros((1, wide_d - model), F32)], axis=1)
    with scope("send3"):
        exchange(part, p3buf, r3buf, 2)
        rest = jnp.concatenate(
            [middle + as_row(bcon_v), jnp.zeros((1, wide_d - model), F32)], axis=1
        )
    with scope("wait3"):
        units_sum = collect(r3buf, 2)

    with scope("send4"):
        result = units_sum + rest
        fbuf[0] = result
        obuf[my_row] = result
        near = []
        for o in offsets:
            opposite = ((o[0] + half) % side, (o[1] + half) % side)
            if (distance(o), o) < (distance(opposite), opposite):
                near.append(o)
        for dx, dy in near:
            other = (lax.rem(cx + dx, side), lax.rem(cy + dy, side))
            for k in (1 - core,) if (dx, dy) == (0, 0) else (0, 1):
                pltpu.make_async_remote_copy(
                    src_ref=fbuf.at[0],
                    dst_ref=obuf.at[my_row],
                    send_sem=send_sem.at[3],
                    recv_sem=recv_sem.at[3],
                    device_id=(seq_of(*other, k), z),
                    device_id_type=MESH,
                ).start()
        wait_all(rbuf, shards - 1, send_sem.at[0])
        wait_all(r2buf, planes - 1, send_sem.at[1])
        wait_all(r3buf, planes - 1, send_sem.at[2])
    with scope("wait4"):
        wait_all(obuf, rows - 1, recv_sem.at[3])
    with scope("finish"):
        for t in range(steps):
            hid_o[t] = obuf[t * requests : (t + 1) * requests, 0, 0:model].astype(BF16)
        wait_all(obuf, rows - 1, send_sem.at[3])


def write_kernel(hid_i, key_i, val_i, hid_o, key_o, val_o, sem):
    pairs = ((key_i, key_o), (val_i, val_o), (hid_i, hid_o))
    copies = [pltpu.make_async_copy(src, dst, sem.at[i]) for i, (src, dst) in enumerate(pairs)]
    for copy in copies:
        copy.start()
    for copy in copies:
        copy.wait()


def per_device(
    side,
    planes,
    tokens,
    first_gain,
    first_shift,
    input_weight,
    input_bias,
    output_weight,
    output_bias,
    second_gain,
    second_shift,
    expand_weight,
    expand_bias,
    contract_weight,
    contract_bias,
    key_cache,
    value_cache,
    cache_fill,
    owner_shard,
):
    steps, requests, model = tokens.shape
    width = input_weight.shape[2]
    units = expand_weight.shape[1]
    slots = key_cache.shape[1]
    rows = steps * requests
    shards = 2 * side * side
    wide_d = -(-model // 128) * 128
    cfg = (side, planes, steps, requests, slots, width, model, units)
    args = (
        tokens,
        first_gain,
        first_shift,
        input_weight.transpose(1, 0, 2),
        input_bias,
        output_weight.T,
        output_bias,
        second_gain,
        second_shift,
        expand_weight.T,
        expand_bias,
        contract_weight,
        contract_bias,
        key_cache,
        value_cache,
        cache_fill,
        owner_shard,
    )
    row = pltpu.VMEM((model,), F32)
    outs = (tokens.shape, key_cache.shape, value_cache.shape)
    results = pl.pallas_call(
        functools.partial(layer_kernel, cfg),
        out_shape=tuple(pltpu.VMEM(shape, BF16) for shape in outs),
        in_specs=[pl.BlockSpec(memory_space=pl.ANY)] * len(args),
        out_specs=tuple(pl.BlockSpec(memory_space=pltpu.VMEM) for _ in outs),
        scratch_shapes=[
            pltpu.VMEM(tokens.shape, BF16),
            row,
            row,
            pltpu.VMEM((3, model, width), BF16),
            pltpu.VMEM((3, width), F32),
            pltpu.VMEM((model, width), BF16),
            row,
            row,
            row,
            pltpu.VMEM((units, model), BF16),
            pltpu.VMEM((units,), F32),
            pltpu.VMEM((units, model), BF16),
            row,
            pltpu.SMEM(cache_fill.shape, jnp.int32),
            pltpu.SMEM(owner_shard.shape, jnp.int32),
            pltpu.VMEM((rows, model), F32),
            pltpu.VMEM((rows, width), F32),
            pltpu.VMEM((rows, width), F32),
            pltpu.VMEM((rows, 1, width + 128), F32),
            pltpu.VMEM((shards, 1, width + 128), F32),
            pltpu.VMEM((1, 1, wide_d), F32),
            pltpu.VMEM((planes, 1, wide_d), F32),
            pltpu.VMEM((1, 1, wide_d), F32),
            pltpu.VMEM((planes, 1, wide_d), F32),
            pltpu.VMEM((1, 1, wide_d), F32),
            pltpu.VMEM((rows, 1, wide_d), F32),
            pltpu.SemaphoreType.DMA((17 + 2 + 2 * (requests - 1),)),
            pltpu.SemaphoreType.DMA((4,)),
            pltpu.SemaphoreType.DMA((4,)),
        ],
        compiler_params=pltpu.CompilerParams(collective_id=0, has_side_effects=True),
        name="layer",
    )(*args)
    return pl.pallas_call(
        write_kernel,
        out_shape=tuple(jax.ShapeDtypeStruct(shape, BF16) for shape in outs),
        in_specs=[pl.BlockSpec(memory_space=pltpu.VMEM)] * len(outs),
        out_specs=tuple(pl.BlockSpec(memory_space=pl.ANY) for _ in outs),
        scratch_shapes=[pltpu.SemaphoreType.DMA((len(outs),))],
        name="write",
    )(*(pltpu.with_memory_space_constraint(r, pltpu.VMEM) for r in results))


def solution(mesh):
    side = math.isqrt(mesh.shape["seq"] // 2)
    return jax.shard_map(
        functools.partial(per_device, side, mesh.shape["tensor"]),
        mesh=mesh,
        in_specs=(
            P(),
            P(),
            P(),
            P(None, None, "tensor"),
            P(None, "tensor"),
            P("tensor", None),
            P(),
            P(),
            P(),
            P(None, "tensor"),
            P("tensor"),
            P("tensor", None),
            P(),
            P(None, "seq", "tensor"),
            P(None, "seq", "tensor"),
            P(),
            P(),
        ),
        out_specs=(P(), P(None, "seq", "tensor"), P(None, "seq", "tensor")),
        check_vma=False,
    )
```

time: 37 us -> 33.2 us (0.90)
  local copies, waits for them, and re-layouts: 4.77 us -> 0 us
  Pallas kernels: 31.5 us -> 32.4 us
    unnamed x4 -> x0, local copies, waits for them, and re-layouts: 3.24 us -> none
    reshape x1 -> x0, local copies, waits for them, and re-layouts: 1.54 us -> none  [per_device(): return (hidden.reshape(steps, requests, model), new_keys, new_values)]
    pallas_call x1 -> x2, Pallas kernels: 31.5 us -> 32.4 us  [the longest x1 31.1 us: per_device(): pl.pallas_call(functools.partial(layer_kernel, cfg), out_shape=tuple((plt...]
where the time goes in v2:
time: 33.2 us; the launch traced here: 33.1 us
  Pallas kernels  32.4 us (98%)
  between operations  0.65 us (2%)
    pallas_call x1, Pallas kernels, per_device(): pl.pallas_call(functools.partial(layer_kernel, cfg), out_shape=tuple((plt...  31.1 us
    pallas_call x1, Pallas kernels, per_device(): pl.pallas_call(write_kernel, out_shape=tuple((jax.ShapeDtypeStruct(shape,...  1.35 us

profile of v2, /device:TPU:1, one launch (start us, length us, event | category | flops | bytes accessed | tf_op | source)
XLA Modules:
  0.0 33.1 jit_solution(12821591158326116111)
XLA Ops:
  0.6 31.1 %layer.1 = (bf16[4,4,1600]{2,1,0:T(4,128)(2,1)S(1)}, bf16[4,512,256]{2,1,0:T(8,128)(2,1)S(1)}, bf16[4,512,256]{2,1,0:T(8,128)(2,1)S(1)}) custom-call(bf16[4,4,1600]{2,1,0:T(4,128)(2,1)} %tok_h.1, f32[1600]{0:T(1024)} %g1_h.1, f32[1600]{0:T(1024)} %s1_h.1, bf16[3,1600,256]{2,1,0:T(8,128)(2,1)} %bitcast.4, f32[3,256]{1,0:T(4,128)} %bin_h.1, ...), custom_call_target="tpu_custom_call" | custom-call | tf_op jit(solution)/shard_map/layer/pallas_call | solution.py:449
  31.7 1.3 %write.1 = (bf16[4,4,1600]{2,1,0:T(4,128)(2,1)}, bf16[4,512,256]{2,1,0:T(8,128)(2,1)}, bf16[4,512,256]{2,1,0:T(8,128)(2,1)}) custom-call(bf16[4,4,1600]{2,1,0:T(4,128)(2,1)S(1)} %get-tuple-element.6.hid_i, bf16[4,512,256]{2,1,0:T(8,128)(2,1)S(1)} %get-tuple-element.7.key_i, bf16[4,512,256]{2,1,0:T(8,128)(2,1)S(1)} %get-tuple-element.8.val_i), custom_call_target="tpu_custom_call" | custom-call | tf_op jit(solution)/shard_map/write/pallas_call | solution.py:488

commit v3 on v2

--- a/solution.py
+++ b/solution.py
@@ -119,12 +119,11 @@
 
     with scope("issue"):
         c_small = [load(tok_h, tok_v), load(g1_h, g1_v), load(s1_h, s1_v)]
-        c_win = [load(win_h.at[0], win_v.at[0])]
+        c_win = load(win_h.at[0], win_v.at[0])
         c_bin = load(bin_h, bin_v)
         c_fill = [load(fill_h, fill_s), load(own_h, own_s)]
-        c_key = [load(key_h.at[b], key_v.at[b]) for b in range(requests)]
-        c_win += [load(win_h.at[1], win_v.at[1]), load(win_h.at[2], win_v.at[2])]
-        c_val = [load(val_h.at[b], val_v.at[b]) for b in range(requests)]
+        c_key = load(key_h, key_v)
+        c_rest = [load(win_h.at[pl.ds(1, 2)], win_v.at[pl.ds(1, 2)]), load(val_h, val_v)]
 
     def distance(o):
         return min(o[0], side - o[0]) + min(o[1], side - o[1])
@@ -140,22 +139,19 @@
         else:
             plane_peers.append((*other, 0))
             plane_peers.append((*other, 1))
-    column_peers = [
-        lax.rem(z + dz, planes)
-        for dz in sorted(range(1, planes), key=lambda d: -min(d, planes - d))
-    ]
+    column_steps = sorted(range(1, planes), key=lambda d: -min(d, planes - d))
+    column_peers = [lax.rem(z + dz, planes) for dz in column_steps]
 
     def seq_of(x, y, k):
         return (x * side + y) * 2 + k
 
     barrier = pltpu.get_barrier_semaphore()
     with scope("signals"):
-        for peer in plane_peers:
-            pl.semaphore_signal(
-                barrier, inc=1, device_id=(seq_of(*peer), z), device_id_type=MESH
-            )
-        for other in column_peers:
-            pl.semaphore_signal(barrier, inc=1, device_id=(shard, other), device_id_type=MESH)
+        hops = [distance(o) for o in offsets for _ in range(2)][: len(plane_peers)]
+        greet = [(h, (seq_of(*peer), z)) for h, peer in zip(hops, plane_peers)]
+        greet += [(min(dz, planes - dz), (shard, o)) for dz, o in zip(column_steps, column_peers)]
+        for _, device in sorted(greet, key=lambda g: -g[0]):
+            pl.semaphore_signal(barrier, inc=1, device_id=device, device_id_type=MESH)
 
     with scope("norm1"):
         for c in c_small:
@@ -165,8 +161,11 @@
         normed = layer_norm(x_v[...], as_row(g1_v), as_row(s1_v)).astype(BF16)
         c_bin.wait()
 
+    with scope("load1"):
+        for c in (c_win, *c_fill, c_key):
+            c.wait()
+
     def project(part):
-        c_win[part].wait()
         return (
             jnp.dot(normed, win_v[part], preferred_element_type=F32) + bin_v[part : part + 1, :]
         ).astype(BF16)
@@ -174,8 +173,6 @@
     with scope("query"):
         query = project(0)
 
-    for c in c_fill:
-        c.wait()
     fills = [fill_s[b, shard] for b in range(requests)]
     owned = [
         [(own_s[t, b] == shard).astype(jnp.int32) for b in range(requests)] for t in range(steps)
@@ -212,9 +209,11 @@
     scores = None
     with scope("scores"):
         for b in range(requests):
-            c_key[b].wait()
             part = dot_nt(query_heads, key_v[b])
             scores = part if scores is None else jnp.where(row_b == b, part, scores)
+    with scope("load2"):
+        for c in c_rest:
+            c.wait()
     with scope("keyvalue"):
         key_new = project(1)
         value_new = project(2)
@@ -235,7 +234,6 @@
         )
         blended = jnp.dot(weights_new.astype(BF16), value_new, preferred_element_type=F32)
         for b in range(requests):
-            c_val[b].wait()
             blended = blended + jnp.dot(
                 jnp.where(row_b == b, weights, 0.0).astype(BF16),
                 val_v[b],
@@ -478,7 +476,7 @@
             pltpu.VMEM((planes, 1, wide_d), F32),
             pltpu.VMEM((1, 1, wide_d), F32),
             pltpu.VMEM((rows, 1, wide_d), F32),
-            pltpu.SemaphoreType.DMA((17 + 2 + 2 * (requests - 1),)),
+            pltpu.SemaphoreType.DMA((18,)),
             pltpu.SemaphoreType.DMA((4,)),
             pltpu.SemaphoreType.DMA((4,)),
         ],

time: 33.2 us -> 33.1 us (level)
  no operation moved by 1% of the time
where the time goes in v3:
time: 33.1 us; the launch traced here: 33 us
  Pallas kernels  32.4 us (98%)
  between operations  0.65 us (2%)
    pallas_call x1, Pallas kernels, per_device(): pl.pallas_call(functools.partial(layer_kernel, cfg), out_shape=tuple((plt...  31 us
    pallas_call x1, Pallas kernels, per_device(): pl.pallas_call(write_kernel, out_shape=tuple((jax.ShapeDtypeStruct(shape,...  1.35 us

profile of v3, /device:TPU:1, one launch (start us, length us, event | category | flops | bytes accessed | tf_op | source)
XLA Modules:
  0.0 33.0 jit_solution(263363581398424425)
XLA Ops:
  0.6 31.0 %layer.1 = (bf16[4,4,1600]{2,1,0:T(4,128)(2,1)S(1)}, bf16[4,512,256]{2,1,0:T(8,128)(2,1)S(1)}, bf16[4,512,256]{2,1,0:T(8,128)(2,1)S(1)}) custom-call(bf16[4,4,1600]{2,1,0:T(4,128)(2,1)} %tok_h.1, f32[1600]{0:T(1024)} %g1_h.1, f32[1600]{0:T(1024)} %s1_h.1, bf16[3,1600,256]{2,1,0:T(8,128)(2,1)} %bitcast.4, f32[3,256]{1,0:T(4,128)} %bin_h.1, ...), custom_call_target="tpu_custom_call" | custom-call | tf_op jit(solution)/shard_map/layer/pallas_call | solution.py:447
  31.7 1.3 %write.1 = (bf16[4,4,1600]{2,1,0:T(4,128)(2,1)}, bf16[4,512,256]{2,1,0:T(8,128)(2,1)}, bf16[4,512,256]{2,1,0:T(8,128)(2,1)}) custom-call(bf16[4,4,1600]{2,1,0:T(4,128)(2,1)S(1)} %get-tuple-element.6.hid_i, bf16[4,512,256]{2,1,0:T(8,128)(2,1)S(1)} %get-tuple-element.7.key_i, bf16[4,512,256]{2,1,0:T(8,128)(2,1)S(1)} %get-tuple-element.8.val_i), custom_call_target="tpu_custom_call" | custom-call | tf_op jit(solution)/shard_map/write/pallas_call | solution.py:486
